TPU v7x, 32 devices: a whole 2x2x4 slice. The times are simulated.
32 devices in a mesh: groups: 2 (over x), expert: 16 (over z, y, core).
Axes of the slice: x: 2, y: 2, z: 4, core: 2. Of those that a mesh axis runs over, the one named last changes fastest.
Arguments:
- residual: bfloat16 [512, 2880], P(('groups', 'expert')), parts along dimension 0, may hold values from -6 to 6
- norm_gain: float32 [2880], replicated, may hold values from 0.1 to 1.9
- expert_ids: int32 [512, 4], P(('groups', 'expert')), parts along dimension 0, may hold values from 0 to 7, all different within a row; in each aligned block of 16 rows (0 to 15, 16 to 31, ...) at most 16 rows name the same one
- expert_weights: float32 [512, 4], P(('groups', 'expert')), parts along dimension 0, may hold values from 0.2 to 1
- gate_proj: bfloat16 [16, 2880, 720], P('expert'), may hold values from -0.109375 to 0.109375
- up_proj: bfloat16 [16, 2880, 720], P('expert'), may hold values from -0.109375 to 0.109375
- down_proj: bfloat16 [16, 720, 2880], P('expert'), may hold values from -0.15625 to 0.15625
Outputs:
- mixed: bfloat16 [512, 2880], P(('groups', 'expert')), parts along dimension 0
There are 2 independent parts, one for each index of `groups`. A program takes and returns all parts, laid end to end along the dimension named above; an argument that names none is the same for every part. Nothing has to cross between parts.
Inputs may be any that keep to these rules, and one draw needn't show every extreme that they name: `expert_ids`: in each aligned block of 16 rows (the rows of one device) no expert is named by more than 16 entries.
All inputs are finite; a program needn't handle non-finite values.
Results may differ from a plain program's by a relative error of at most 0.0063.
Values may be sent and summed in bfloat16 or wider, within the bound.
A program may use at most 64 MiB of HBM per device.

v0:
```python
import jax
import jax.numpy as jnp
from jax import lax
from jax.sharding import PartitionSpec as P


def partner(value, axis, bit):
    mask = 2**bit
    pairs = [(source, source ^ mask) for source in range(lax.axis_size(axis))]
    return lax.ppermute(value, axis, pairs)


def expert_half(block, gate_w, up_w, down_w):
    flat = block.reshape(-1, block.shape[-1])
    gate = jnp.dot(flat, gate_w, preferred_element_type=jnp.float32)
    upper = jnp.dot(flat, up_w, preferred_element_type=jnp.float32)
    act = (gate * jax.nn.sigmoid(1.702 * gate) * (upper + 1.0)).astype(jnp.bfloat16)
    out = jnp.dot(act, down_w, preferred_element_type=jnp.float32).astype(jnp.bfloat16)
    return out.reshape(block.shape[:-1] + (down_w.shape[1],))


def body(residual, norm_gain, expert_ids, expert_weights, gate_proj, up_proj, down_proj):
    rows, model = residual.shape
    chosen = expert_ids.shape[1]
    devices = lax.axis_size("expert")
    experts = devices // 2
    capacity = 2 * rows * chosen // experts
    half_cap = capacity // 2
    gate_w, up_w, down_w = (gate_proj[0], up_proj[0], down_proj[0])
    x = residual.astype(jnp.float32)
    scale = lax.rsqrt(jnp.mean(x * x, axis=-1, keepdims=True) + 1e-05)
    normed = (x * scale * norm_gain).astype(jnp.bfloat16)
    flat_ids = expert_ids.reshape(rows * chosen)
    onehot = (
        flat_ids[:, None] == lax.broadcasted_iota(jnp.int32, (rows * chosen, experts), 1)
    ).astype(jnp.int32)
    slot = jnp.sum(onehot * jnp.cumsum(onehot, axis=0), axis=1) - 1
    position = flat_ids * capacity + slot
    pick = (
        position[:, None] == lax.broadcasted_iota(jnp.int32, (rows * chosen, experts * capacity), 1)
    ).astype(jnp.float32)
    place_rows = jnp.sum(pick.reshape(rows, chosen, experts * capacity), axis=1)
    send = lax.dot_general(
        place_rows.astype(jnp.bfloat16),
        normed,
        (((0,), (0,)), ((), ())),
        preferred_element_type=jnp.float32,
    )
    send = send.astype(jnp.bfloat16).reshape(experts, capacity, model)
    outgoing = send.reshape(experts, 2, half_cap, model).reshape(devices, half_cap, model)
    arrived = lax.all_to_all(outgoing, "expert", split_axis=0, concat_axis=0, tiled=True)
    other = partner(arrived, "expert", 0)
    both = expert_half(jnp.stack((arrived, other)), gate_w, up_w, down_w)
    returned = partner(both[1], "expert", 0)
    finished = (both[0].astype(jnp.float32) + returned.astype(jnp.float32)).astype(jnp.bfloat16)
    back = lax.all_to_all(finished, "expert", split_axis=0, concat_axis=0, tiled=True)
    results = back.reshape(experts, capacity, model)
    weighted = jnp.sum(
        (pick * expert_weights.reshape(rows * chosen)[:, None]).reshape(
            rows, chosen, experts * capacity
        ),
        axis=1,
    )
    combined = jnp.dot(
        weighted,
        results.reshape(experts * capacity, model).astype(jnp.float32),
        precision=lax.Precision.HIGHEST,
    )
    return (x + combined).astype(jnp.bfloat16)


def solution(mesh):
    in_specs = (
        P(("groups", "expert"), None),
        P(),
        P(("groups", "expert"), None),
        P(("groups", "expert"), None),
        P("expert", None, None),
        P("expert", None, None),
        P("expert", None, None),
    )
    out_specs = P(("groups", "expert"), None)
    return jax.shard_map(body, mesh=mesh, in_specs=in_specs, out_specs=out_specs, check_vma=False)
```

profile of v0, /device:TPU:0, one launch (start us, length us, event | category | flops | bytes accessed | tf_op | source)
XLA Modules:
  0.0 76.8 jit_solution(909006792527382461)
XLA Ops:
  0.0 0.8 copy.23
  0.8 0.1 eq.20
  0.8 0.1 fusion.27
  0.9 0.1 reduce_window_sum.11
  1.0 0.2 select_reduce_fusion.1
  1.2 0.1 sub.7
  1.3 0.1 copy.24
  1.4 0.7 multiply_add_fusion
  2.1 1.0 %fusion.21 = f32[16]{0:T(128)S(1)} fusion(bf16[16,2880]{1,0:T(8,128)(2,1)} %param.7), kind=kLoop, calls=%fused_computation.21 | loop fusion | flops 138224 | bytes 92224 | tf_op jit(solution)/shard_map/reduce_sum | solution.py:31
  3.1 0.8 %convert_reduce_fusion = (bf16[16,128]{1,0:T(8,128)(2,1)S(1)}, f32[16,128]{1,0:T(8,128)S(1)}) fusion(s32[16,4]{0,1:T(4,128)S(1)} %multiply_add_fusion, f32[16,4]{0,1:T(4,128)} %param.10), kind=kLoop, calls=%fused_computation.26 | loop fusion | flops 36864 | bytes 12800 | tf_op jit(solution)/shard_map/reduce_sum | solution.py:42
  3.9 1.4 %convolution_convert_fusion = bf16[128,2880]{0,1:T(8,128)(2,1)S(1)} fusion(bf16[16,2880]{1,0:T(8,128)(2,1)} %param.7, f32[2880]{0:T(1024)} %param.8, f32[16]{0:T(128)S(1)} %add_rsqrt_fusion, bf16[16,128]{1,0:T(8,128)(2,1)S(1)} %get-tuple-element.5), kind=kOutput, calls=%fused_computation.7 | convolution fusion | flops 12349440 | bytes 845120 | tf_op jit(solution)/shard_map/dot_general | solution.py:43
  5.3 0.4 copy.25
  5.7 0.0 copy-start.1
  5.7 27.0 %all_to_all.10 = bf16[16,8,2880]{2,1,0:T(8,128)(2,1)S(1)} all-to-all(bf16[16,8,2880]{2,1,0:T(8,128)(2,1)S(1)} %bitcast.34), channel_id=1, replica_groups=mesh['groups'=2,'expert'=16] {'expert'}, dimensions={0} | all-to-all | bytes 1474560 | tf_op jit(solution)/shard_map/all_to_all | solution.py:51
  32.7 0.9 %collective-permute-start = (bf16[16,8,2880]{2,1,0:T(8,128)(2,1)S(1)}, bf16[16,8,2880]{2,1,0:T(8,128)(2,1)S(1)}, u32[]{:S(2)}, u32[]{:S(2)}) collective-permute-start(bf16[16,8,2880]{2,1,0:T(8,128)(2,1)S(1)} %all_to_all.10), channel_id=1, source_target_pairs={{0,1},{1,0},{2,3},{3,2},{4,5},{5,4},{6,7},{7,6},{8,9},{9,8},{10,11... | collective-permute-start | bytes 2211848 | tf_op jit(solution)/shard_map/ppermute | solution.py:10
  33.5 1.9 %collective-permute-done = bf16[16,8,2880]{2,1,0:T(8,128)(2,1)S(1)} collective-permute-done((bf16[16,8,2880]{2,1,0:T(8,128)(2,1)S(1)}, bf16[16,8,2880]{2,1,0:T(8,128)(2,1)S(1)}, u32[]{:S(2)}, u32[]{:S(2)}) %collective-permute-start) | collective-permute-done | bytes 737312 | tf_op jit(solution)/shard_map/ppermute | solution.py:10
  35.4 0.2 pad_maximum_fusion
  35.6 0.0 copy-done.1
  35.6 1.3 %fusion.4 = f32[256,720]{0,1:T(8,128)S(1)} fusion(bf16[256,2880]{1,0:T(8,128)(2,1)S(1)} %bitcast.35, bf16[1,2880,720]{1,2,0:T(8,128)(2,1)S(1)} %copy-done.1), kind=kOutput, calls=%fused_computation.4 | convolution fusion | flops 1061683200 | bytes 6359040 | tf_op jit(solution)/shard_map/dot_general | solution.py:15
  36.9 9.4 %fusion.6 = bf16[256,2880]{0,1:T(8,128)(2,1)} fusion(bf16[1,720,2880]{2,1,0:T(8,128)(2,1)} %param.13, f32[256,720]{0,1:T(8,128)S(1)} %fusion.4, bf16[256,2880]{1,0:T(8,128)(2,1)S(1)} %bitcast.36, bf16[1,2880,720]{1,2,0:T(8,128)(2,1)} %param.12), kind=kOutput, calls=%fused_computation.6 | convolution fusion | flops 2125578240 | bytes 11980800 | tf_op jit(solution)/shard_map/dot_general | solution.py:18
  46.3 1.5 %fusion.31 = (bf16[128,2880]{0,1:T(8,128)(2,1)S(1)}, f32[128,2880]{0,1:T(8,128)S(1)}) fusion(bf16[256,2880]{0,1:T(8,128)(2,1)} %fusion.6), kind=kLoop, calls=%fused_computation.38 | loop fusion | flops 368640 | bytes 3686400 | tf_op jit(solution)/shard_map/slice | solution.py:54
  47.8 1.2 %copy.27 = bf16[128,2880]{1,0:T(8,128)(2,1)} copy(bf16[128,2880]{0,1:T(8,128)(2,1)S(1)} %get-tuple-element.7) | data formatting | bytes 1474560 | tf_op jit(solution)/shard_map/slice | solution.py:54
  49.0 0.4 collective-permute-start.1
  49.4 0.5 copy.26
  49.8 1.7 %collective-permute-done.1 = bf16[16,8,2880]{2,1,0:T(8,128)(2,1)} collective-permute-done((bf16[16,8,2880]{2,1,0:T(8,128)(2,1)}, bf16[16,8,2880]{2,1,0:T(8,128)(2,1)}, u32[]{:S(2)}, u32[]{:S(2)}) %collective-permute-start.1) | collective-permute-done | bytes 737312 | tf_op jit(solution)/shard_map/ppermute | solution.py:10
  51.6 1.3 %fusion.10 = bf16[16,8,2880]{2,1,0:T(8,128)(2,1)S(1)} fusion(f32[128,2880]{1,0:T(8,128)S(1)} %copy.26, bf16[16,8,2880]{2,1,0:T(8,128)(2,1)} %collective-permute-done.1), kind=kLoop, calls=%fused_computation.12 | loop fusion | flops 1105920 | bytes 2949120 | tf_op jit(solution)/shard_map/convert_element_type | solution.py:55
  52.9 0.0 copy-start
  52.9 22.8 %all_to_all.11 = bf16[16,8,2880]{2,1,0:T(8,128)(2,1)S(1)} all-to-all(bf16[16,8,2880]{2,1,0:T(8,128)(2,1)S(1)} %fusion.10), channel_id=1, replica_groups=mesh['groups'=2,'expert'=16] {'expert'}, dimensions={0} | all-to-all | bytes 1474560 | tf_op jit(solution)/shard_map/all_to_all | solution.py:56
  75.7 0.0 copy-done
  75.7 1.1 %fusion.9 = bf16[16,2880]{1,0:T(8,128)(2,1)} fusion(f32[16,128]{1,0:T(8,128)S(1)} %get-tuple-element.6, bf16[16,8,2880]{2,1,0:T(8,128)(2,1)S(1)} %all_to_all.11, bf16[16,2880]{1,0:T(8,128)(2,1)S(1)} %copy-done), kind=kOutput, calls=%fused_computation.9 | convolution fusion | flops 70917120 | bytes 929792 | tf_op jit(solution)/shard_map/dot_general | solution.py:64
  (2 shorter events, 0.0 us)
Async XLA Ops:
  5.7 29.9 %copy-start.1 = (bf16[1,2880,720]{1,2,0:T(8,128)(2,1)S(1)}, bf16[1,2880,720]{1,2,0:T(8,128)(2,1)}, u32[]{:S(2)}) copy-start(bf16[1,2880,720]{1,2,0:T(8,128)(2,1)} %param.11) | copy-start | bytes 12441604
  32.7 2.7 %collective-permute-start = (bf16[16,8,2880]{2,1,0:T(8,128)(2,1)S(1)}, bf16[16,8,2880]{2,1,0:T(8,128)(2,1)S(1)}, u32[]{:S(2)}, u32[]{:S(2)}) collective-permute-start(bf16[16,8,2880]{2,1,0:T(8,128)(2,1)S(1)} %all_to_all.10), channel_id=1, source_target_pairs={{0,1},{1,0},{2,3},{3,2},{4,5},{5,4},{6,7},{7,6},{8,9},{9,8},{10,11... | collective-permute-start | bytes 2211848 | tf_op jit(solution)/shard_map/ppermute | solution.py:10
  49.0 2.6 %collective-permute-start.1 = (bf16[16,8,2880]{2,1,0:T(8,128)(2,1)}, bf16[16,8,2880]{2,1,0:T(8,128)(2,1)}, u32[]{:S(2)}, u32[]{:S(2)}) collective-permute-start(bf16[16,8,2880]{2,1,0:T(8,128)(2,1)} %bitcast.8), channel_id=1, source_target_pairs={{0,1},{1,0},{2,3},{3,2},{4,5},{5,4},{6,7},{7,6},{8,9},{9,8},{10,11... | collective-permute-start | bytes 2211848 | tf_op jit(solution)/shard_map/ppermute | solution.py:10
  52.9 22.8 %copy-start = (bf16[16,2880]{1,0:T(8,128)(2,1)S(1)}, bf16[16,2880]{1,0:T(8,128)(2,1)}, u32[]{:S(2)}) copy-start(bf16[16,2880]{1,0:T(8,128)(2,1)} %param.7) | copy-start | bytes 276484
where the time goes:
time: 77.5 us; the launch traced here: 76.8 us
  blocking collectives  49.8 us (64%)
  matrix products  13.2 us (17%)
  other arithmetic  5.79 us (7%)
  waiting for transfers between devices  3.61 us (5%)
  local copies, waits for them, and re-layouts  3.03 us (4%)
  starting transfers between devices  1.24 us (2%)
    all_to_all x1, blocking collectives, body(): lax.all_to_all(outgoing, 'expert', split_axis=0, concat_axis=0, tiled=True)  27 us
    all_to_all x1, blocking collectives, body(): lax.all_to_all(finished, 'expert', split_axis=0, concat_axis=0, tiled=True)  22.8 us
    dot_general x1, matrix products, expert_half(): jnp.dot(act, down_w, preferred_element_type=jnp.float32)  9.39 us
    ppermute x2, waiting for transfers between devices, partner(): return lax.ppermute(value, axis, pairs)  3.61 us
  transfers between devices with their start and end apart: 2, of which 2 were waited for; matrix products, arithmetic and copies ran while one was open for 1% of the time, Pallas kernels for 0%

commit v1 on v0

--- a/solution.py
+++ b/solution.py
@@ -1,7 +1,15 @@
+import functools
+
 import jax
 import jax.numpy as jnp
 from jax import lax
+from jax.experimental import pallas as pl
+from jax.experimental.pallas import tpu as pltpu
 from jax.sharding import PartitionSpec as P
+
+BF16 = jnp.bfloat16
+F32 = jnp.float32
+LANES = 128
 
 
 def partner(value, axis, bit):
@@ -19,7 +27,7 @@
     return out.reshape(block.shape[:-1] + (down_w.shape[1],))
 
 
-def body(residual, norm_gain, expert_ids, expert_weights, gate_proj, up_proj, down_proj):
+def slotted(residual, norm_gain, expert_ids, expert_weights, gate_proj, up_proj, down_proj):
     rows, model = residual.shape
     chosen = expert_ids.shape[1]
     devices = lax.axis_size("expert")
@@ -69,6 +77,291 @@
     return (x + combined).astype(jnp.bfloat16)
 
 
+def cuts(total, pieces):
+    step = -(-total // (pieces * 2 * LANES)) * 2 * LANES
+    return [(start, min(step, total - start)) for start in range(0, total, step)]
+
+
+def kernel(
+    line, experts, in_cuts, out_cuts,
+    res_ref, gain_ref, ids_ref, wts_ref, gate_hbm, up_hbm, down_hbm, out_ref,
+    gate_v, up_v, down_v, xg, gacc, uacc, part, core_r, y_s, y_r, z_s, z_r,
+    w_sem, d_sem, agz_s, agz_r, agy_s, agy_r, agc_s, agc_r,
+    rc_s, rc_r, ry_s, ry_r, rz_s, rz_r,
+):
+    rows, model = res_ref.shape
+    extra = xg.shape[1] - model
+    me = lax.axis_index("expert")
+    core = lax.rem(me, 2)
+    y = lax.rem(me // 2, 2)
+    z = me // 4
+
+    def device(z_, y_, c_):
+        return (z_ * 2 + y_) * 2 + c_
+
+    def row(z_, y_, c_):
+        return pl.multiple_of(((c_ * 2 + y_) * line + z_) * rows, rows)
+
+    def z_at(offset):
+        return lax.rem(z + offset + line, line)
+
+    def remote(src, dst, send, recv, target):
+        return pltpu.make_async_remote_copy(
+            src_ref=src, dst_ref=dst, send_sem=send, recv_sem=recv,
+            device_id={"expert": target}, device_id_type=pl.DeviceIdType.MESH,
+        )
+
+    y_dev = device(z, 1 - y, core)
+    c_dev = device(z, y, 1 - core)
+
+    loads = []
+    for k, (at, wide) in enumerate(in_cuts):
+        pair = []
+        for n, (hbm, vmem) in enumerate(((gate_hbm, gate_v), (up_hbm, up_v))):
+            copy = pltpu.make_async_copy(
+                hbm.at[0, pl.ds(at, wide), :], vmem.at[pl.ds(at, wide), :], w_sem.at[k, n]
+            )
+            copy.start()
+            pair.append(copy)
+        loads.append(pair)
+    down_load = pltpu.make_async_copy(down_hbm.at[0], down_v, d_sem)
+    down_load.start()
+
+    barrier = pltpu.get_barrier_semaphore()
+    peers = [device(z_at(o), y, core) for o in range(1, line)] + [y_dev, c_dev]
+    for peer in peers:
+        pl.semaphore_signal(
+            barrier, inc=1, device_id={"expert": peer}, device_id_type=pl.DeviceIdType.MESH
+        )
+
+    mine = row(z, y, core)
+    x = res_ref[...].astype(F32)
+    scale = lax.rsqrt(jnp.mean(x * x, axis=-1, keepdims=True) + 1e-05)
+    xg[pl.ds(mine, rows), 0:model] = (x * scale * gain_ref[...]).astype(BF16)
+    lane = lax.broadcasted_iota(jnp.int32, (rows, extra), 1)
+    high = jnp.zeros((rows, extra), F32)
+    low = jnp.zeros((rows, extra), F32)
+    for k in range(ids_ref.shape[1]):
+        ids = ids_ref[:, k : k + 1]
+        high = high + jnp.where(ids == lane, wts_ref[:, k : k + 1], 0.0)
+        low = low + jnp.where(ids + experts == lane, wts_ref[:, k : k + 1], 0.0)
+    rest = low - low.astype(BF16).astype(F32)
+    xg[pl.ds(mine, rows), model : model + extra] = (high + rest).astype(BF16)
+
+    pl.semaphore_wait(barrier, len(peers))
+
+    sent = []
+
+    def go(copy):
+        copy.start()
+        sent.append(copy)
+
+    spans = []
+    for k, (at, wide) in enumerate(in_cuts):
+        if k == len(in_cuts) - 1:
+            wide = wide + extra
+        spans.append((at, wide))
+
+    def block(z_, y_, c_, count, k):
+        at, wide = spans[k]
+        return xg.at[pl.ds(row(z_, y_, c_), count * rows), pl.ds(at, wide)]
+
+    chunks = len(in_cuts)
+    for k in range(chunks):
+        own = block(z, y, core, 1, k)
+        for o in range(1, line):
+            go(remote(own, own, agz_s.at[k, o], agz_r.at[k, o], device(z_at(o), y, core)))
+        go(remote(own, own, agy_s.at[k, 0], agy_r.at[k, 0], y_dev))
+
+    def relay_z(k):
+        for o in range(1, line):
+            got = block(z_at(-o), y, core, 1, k)
+            remote(got, got, agz_s.at[k, o], agz_r.at[k, o], me).wait_recv()
+            go(remote(got, got, agy_s.at[k, o], agy_r.at[k, o], y_dev))
+        group = block(0, y, core, line, k)
+        go(remote(group, group, agc_s.at[k, 0], agc_r.at[k, 0], c_dev))
+
+    def relay_y(k):
+        for o in range(line):
+            got = block(z_at(-o), 1 - y, core, 1, k)
+            remote(got, got, agy_s.at[k, o], agy_r.at[k, o], y_dev).wait_recv()
+        group = block(0, 1 - y, core, line, k)
+        go(remote(group, group, agc_s.at[k, 1], agc_r.at[k, 1], c_dev))
+
+    def arrive(k):
+        for n, y_ in enumerate((y, 1 - y)):
+            group = block(0, y_, 1 - core, line, k)
+            remote(group, group, agc_s.at[k, n], agc_r.at[k, n], c_dev).wait_recv()
+
+    def multiply(k):
+        at, wide = in_cuts[k]
+        tokens = xg[:, at : at + wide]
+        for n, (vmem, acc) in enumerate(((gate_v, gacc), (up_v, uacc))):
+            loads[k][n].wait()
+            product = jnp.dot(tokens, vmem[at : at + wide, :], preferred_element_type=F32)
+            if k == 0:
+                acc[...] = product
+            else:
+                acc[...] += product
+
+    relay_z(0)
+    for k in range(chunks):
+        relay_y(k)
+        if k + 1 < chunks:
+            relay_z(k + 1)
+        arrive(k)
+        multiply(k)
+
+    gate = gacc[...]
+    act = (gate * jax.nn.sigmoid(1.702 * gate) * (uacc[...] + 1.0)).astype(BF16)
+    expert = me // 2
+    lanes = lax.broadcasted_iota(jnp.int32, (xg.shape[0], extra), 1)
+    ours = jnp.logical_or(lanes == expert, lanes == expert + experts)
+    weight = jnp.sum(
+        jnp.where(ours, xg[:, model : model + extra].astype(F32), 0.0), axis=1, keepdims=True
+    )
+    down_load.wait()
+
+    half = 2 * line * rows
+    quarter = line * rows
+    my_half = pl.multiple_of(core * half, half)
+    its_half = pl.multiple_of((1 - core) * half, half)
+    my_y = pl.multiple_of(y * quarter, quarter)
+    its_y = pl.multiple_of((1 - y) * quarter, quarter)
+    my_z = pl.multiple_of(z * rows, rows)
+
+    def core_copy(j):
+        at, wide = out_cuts[j]
+        cols = pl.ds(at, wide)
+        return remote(
+            part.at[pl.ds(its_half, half), cols], core_r.at[:, cols],
+            rc_s.at[j], rc_r.at[j], c_dev,
+        )
+
+    def y_copy(j):
+        at, wide = out_cuts[j]
+        cols = pl.ds(at, wide)
+        return remote(y_s.at[:, cols], y_r.at[:, cols], ry_s.at[j], ry_r.at[j], y_dev)
+
+    def z_copy(j, o):
+        at, wide = out_cuts[j]
+        cols = pl.ds(at, wide)
+        there = pl.multiple_of(z_at(o) * rows, rows)
+        return remote(
+            z_s.at[pl.ds(there, rows), cols], z_r.at[o, :, cols],
+            rz_s.at[j, o], rz_r.at[j, o], device(z_at(o), y, core),
+        )
+
+    def first(j):
+        at, wide = out_cuts[j]
+        product = jnp.dot(act, down_v[:, at : at + wide], preferred_element_type=F32)
+        part[:, at : at + wide] = (product * weight).astype(BF16)
+        go(core_copy(j))
+
+    def second(j):
+        at, wide = out_cuts[j]
+        core_copy(j).wait_recv()
+        theirs = core_r[pl.ds(its_y, quarter), at : at + wide].astype(F32)
+        here = part[pl.ds(my_half + its_y, quarter), at : at + wide].astype(F32)
+        y_s[:, at : at + wide] = (theirs + here).astype(BF16)
+        go(y_copy(j))
+
+    def third(j):
+        at, wide = out_cuts[j]
+        theirs = core_r[pl.ds(my_y, quarter), at : at + wide].astype(F32)
+        here = part[pl.ds(my_half + my_y, quarter), at : at + wide].astype(F32)
+        y_copy(j).wait_recv()
+        total = theirs + here + y_r[:, at : at + wide].astype(F32)
+        z_s[:, at : at + wide] = total.astype(BF16)
+        for o in range(1, line):
+            go(z_copy(j, o))
+
+    def fourth(j):
+        at, wide = out_cuts[j]
+        total = z_s[pl.ds(my_z, rows), at : at + wide].astype(F32)
+        for o in range(1, line):
+            z_copy(j, o).wait_recv()
+            total = total + z_r[o, :, at : at + wide].astype(F32)
+        out_ref[:, at : at + wide] = (
+            res_ref[:, at : at + wide].astype(F32) + total
+        ).astype(BF16)
+
+    pieces = len(out_cuts)
+    for step in range(pieces + 3):
+        for lag, stage in enumerate((first, second, third, fourth)):
+            if 0 <= step - lag < pieces:
+                stage(step - lag)
+    for copy in sent:
+        copy.wait_send()
+
+
+def fused(residual, norm_gain, expert_ids, expert_weights, gate_proj, up_proj, down_proj):
+    rows, model = residual.shape
+    hidden = gate_proj.shape[2]
+    devices = lax.axis_size("expert")
+    experts = devices // 2
+    line = devices // 4
+    tokens = rows * devices
+    width = -(-(model + 2 * experts) // LANES) * LANES
+    in_cuts = cuts(model, 3)
+    out_cuts = cuts(model, 3)
+    ins, outs = len(in_cuts), len(out_cuts)
+    vmem = pl.BlockSpec(memory_space=pltpu.VMEM)
+    hbm = pl.BlockSpec(memory_space=pl.ANY)
+    dma = pltpu.SemaphoreType.DMA
+    return pl.pallas_call(
+        functools.partial(kernel, line, experts, in_cuts, out_cuts),
+        out_shape=jax.ShapeDtypeStruct((rows, model), BF16),
+        in_specs=[vmem] * 4 + [hbm] * 3,
+        out_specs=vmem,
+        scratch_shapes=[
+            pltpu.VMEM((model, hidden), BF16),
+            pltpu.VMEM((model, hidden), BF16),
+            pltpu.VMEM((hidden, model), BF16),
+            pltpu.VMEM((tokens, width), BF16),
+            pltpu.VMEM((tokens, hidden), F32),
+            pltpu.VMEM((tokens, hidden), F32),
+            pltpu.VMEM((tokens, model), BF16),
+            pltpu.VMEM((tokens // 2, model), BF16),
+            pltpu.VMEM((tokens // 4, model), BF16),
+            pltpu.VMEM((tokens // 4, model), BF16),
+            pltpu.VMEM((tokens // 4, model), BF16),
+            pltpu.VMEM((line, rows, model), BF16),
+            dma((ins, 2)),
+            dma,
+            dma((ins, line)),
+            dma((ins, line)),
+            dma((ins, line)),
+            dma((ins, line)),
+            dma((ins, 2)),
+            dma((ins, 2)),
+            dma((outs,)),
+            dma((outs,)),
+            dma((outs,)),
+            dma((outs,)),
+            dma((outs, line)),
+            dma((outs, line)),
+        ],
+        compiler_params=pltpu.CompilerParams(
+            collective_id=0, has_side_effects=True, vmem_limit_bytes=60 * 1024 * 1024
+        ),
+    )(
+        residual, norm_gain.reshape(1, model), expert_ids, expert_weights,
+        gate_proj, up_proj, down_proj,
+    )
+
+
+def body(residual, norm_gain, expert_ids, expert_weights, gate_proj, up_proj, down_proj):
+    rows = residual.shape[0]
+    devices = lax.axis_size("expert")
+    capacity = 4 * rows * expert_ids.shape[1] // devices
+    dense = capacity >= rows and devices % 4 == 0
+    form = fused if dense else slotted
+    return form(
+        residual, norm_gain, expert_ids, expert_weights, gate_proj, up_proj, down_proj
+    )
+
+
 def solution(mesh):
     in_specs = (
         P(("groups", "expert"), None),

time: 77.5 us -> 63.1 us (0.81)
  blocking collectives: 49.8 us -> 0 us
  Pallas kernels: 0 us -> 44 us
  local copies, waits for them, and re-layouts: 3.03 us -> 18.6 us
  matrix products: 13.2 us -> 0 us
  other arithmetic: 5.79 us -> 0 us
  waiting for transfers between devices: 3.61 us -> 0 us
  starting transfers between devices: 1.24 us -> 0 us
    all_to_all x2 -> x0, blocking collectives: 49.8 us -> none  [the longest x1 27 us: body(): lax.all_to_all(outgoing, 'expert', split_axis=0, concat_axis=0, tiled=True)]
    pallas_call x0 -> x1, Pallas kernels: none -> 44 us  [fused(): pl.pallas_call(functools.partial(kernel, line, experts, in_cuts, out_cuts...]
    unnamed x5, local copies, waits for them, and re-layouts: 0.77 us -> 17.3 us
    dot_general x4 -> x0, matrix products: 13.2 us -> none  [the longest x1 9.39 us: expert_half(): jnp.dot(act, down_w, preferred_element_type=jnp.float32)]
    ppermute x2 -> x0, waiting for transfers between devices: 3.61 us -> none  [partner(): return lax.ppermute(value, axis, pairs)]
    reduce_sum x3 -> x0, other arithmetic: 1.97 us -> none  [the longest x1 1.03 us: body(): scale = lax.rsqrt(jnp.mean(x * x, axis=-1, keepdims=True) + 1e-05)]
    slice x1 -> x0, other arithmetic: 1.48 us -> none  [body(): returned = partner(both[1], 'expert', 0)]
    convert_element_type x2 -> x0, other arithmetic: 1.36 us -> none  [the longest x1 1.29 us: body(): (both[0].astype(jnp.float32) + returned.astype(jnp.float32)).astype(jnp.b...]
  transfers between devices with their start and end apart: 2 -> 0, of which waited for: 2 -> 0; matrix products, arithmetic and copies ran while one was open for 1% -> 0% of each run, Pallas kernels for 0% -> 0%
where the time goes in v1:
time: 63.1 us; the launch traced here: 62.6 us
  Pallas kernels  44 us (70%)
  local copies, waits for them, and re-layouts  18.6 us (29%)
    pallas_call x1, Pallas kernels, fused(): pl.pallas_call(functools.partial(kernel, line, experts, in_cuts, out_cuts...  44 us
    unnamed x5, local copies, waits for them, and re-layouts  17.3 us
    reshape x1, local copies, waits for them, and re-layouts, fused(): norm_gain.reshape(1, model)  1.31 us

profile of v1, /device:TPU:0, one launch (start us, length us, event | category | flops | bytes accessed | tf_op | source)
XLA Modules:
  0.0 62.6 jit_solution(7417397296921386492)
XLA Ops:
  0.0 1.3 %copy.8.ids_ref = s32[16,4]{1,0:T(8,128)} copy(s32[16,4]{0,1:T(4,128)} %param.9) | data formatting | bytes 512 | tf_op args[2]
  1.4 1.4 %copy.9.wts_ref = f32[16,4]{1,0:T(8,128)} copy(f32[16,4]{0,1:T(4,128)} %param.10) | data formatting | bytes 512 | tf_op args[3]
  2.7 1.3 %reshape.3.gain_ref = f32[1,2880]{1,0:T(1,128)} reshape(f32[2880]{0:T(1024)} %param.8) | data formatting | bytes 23040 | tf_op jit(solution)/shard_map/reshape | solution.py:349
  4.0 6.5 %copy.10.gate_hbm = bf16[1,2880,720]{2,1,0:T(8,128)(2,1)} copy(bf16[1,2880,720]{1,2,0:T(8,128)(2,1)} %param.11) | data formatting | bytes 8294400 | tf_op args[4]
  10.5 6.5 %copy.11.up_hbm = bf16[1,2880,720]{2,1,0:T(8,128)(2,1)} copy(bf16[1,2880,720]{1,2,0:T(8,128)(2,1)} %param.12) | data formatting | bytes 8294400 | tf_op args[5]
  17.0 44.0 %shard_map.73 = bf16[16,2880]{1,0:T(8,128)(2,1)} custom-call(bf16[16,2880]{1,0:T(8,128)(2,1)} %res_ref.1, f32[1,2880]{1,0:T(1,128)} %reshape.3.gain_ref, s32[16,4]{1,0:T(8,128)} %copy.8.ids_ref, f32[16,4]{1,0:T(8,128)} %copy.9.wts_ref, bf16[1,2880,720]{2,1,0:T(8,128)(2,1)} %copy.10.gate_hbm, bf16[1,2880,720]{2,1,0:T(8,128)(2,1)} %copy.11.up_hbm, ...), custom_call_target="tpu_custom_call" | custom-call | tf_op jit(solution)/shard_map/pallas_call | solution.py:312
  61.1 1.5 %copy.13 = bf16[16,2880]{1,0:T(8,128)(2,1)} copy(bf16[16,2880]{1,0:T(8,128)(2,1)} %shard_map.73) | data formatting | bytes 184320

commit v2 on v1

--- a/solution.py
+++ b/solution.py
@@ -119,7 +119,7 @@
         pair = []
         for n, (hbm, vmem) in enumerate(((gate_hbm, gate_v), (up_hbm, up_v))):
             copy = pltpu.make_async_copy(
-                hbm.at[0, pl.ds(at, wide), :], vmem.at[pl.ds(at, wide), :], w_sem.at[k, n]
+                hbm.at[0, :, pl.ds(at, wide)], vmem.at[:, pl.ds(at, wide)], w_sem.at[k, n]
             )
             copy.start()
             pair.append(copy)
@@ -138,15 +138,15 @@
     x = res_ref[...].astype(F32)
     scale = lax.rsqrt(jnp.mean(x * x, axis=-1, keepdims=True) + 1e-05)
     xg[pl.ds(mine, rows), 0:model] = (x * scale * gain_ref[...]).astype(BF16)
-    lane = lax.broadcasted_iota(jnp.int32, (rows, extra), 1)
-    high = jnp.zeros((rows, extra), F32)
-    low = jnp.zeros((rows, extra), F32)
-    for k in range(ids_ref.shape[1]):
-        ids = ids_ref[:, k : k + 1]
-        high = high + jnp.where(ids == lane, wts_ref[:, k : k + 1], 0.0)
-        low = low + jnp.where(ids + experts == lane, wts_ref[:, k : k + 1], 0.0)
+    named = lax.broadcasted_iota(jnp.int32, (extra, rows), 0)
+    high = jnp.zeros((extra, rows), F32)
+    low = jnp.zeros((extra, rows), F32)
+    for k in range(ids_ref.shape[0]):
+        ids = ids_ref[k : k + 1, :]
+        high = high + jnp.where(ids == named, wts_ref[k : k + 1, :], 0.0)
+        low = low + jnp.where(ids + experts == named, wts_ref[k : k + 1, :], 0.0)
     rest = low - low.astype(BF16).astype(F32)
-    xg[pl.ds(mine, rows), model : model + extra] = (high + rest).astype(BF16)
+    xg[pl.ds(mine, rows), model : model + extra] = jnp.transpose(high + rest).astype(BF16)
 
     pl.semaphore_wait(barrier, len(peers))
 
@@ -198,7 +198,10 @@
         tokens = xg[:, at : at + wide]
         for n, (vmem, acc) in enumerate(((gate_v, gacc), (up_v, uacc))):
             loads[k][n].wait()
-            product = jnp.dot(tokens, vmem[at : at + wide, :], preferred_element_type=F32)
+            product = lax.dot_general(
+                tokens, vmem[:, at : at + wide], (((1,), (1,)), ((), ())),
+                preferred_element_type=F32,
+            )
             if k == 0:
                 acc[...] = product
             else:
@@ -315,8 +318,8 @@
         in_specs=[vmem] * 4 + [hbm] * 3,
         out_specs=vmem,
         scratch_shapes=[
-            pltpu.VMEM((model, hidden), BF16),
-            pltpu.VMEM((model, hidden), BF16),
+            pltpu.VMEM((hidden, model), BF16),
+            pltpu.VMEM((hidden, model), BF16),
             pltpu.VMEM((hidden, model), BF16),
             pltpu.VMEM((tokens, width), BF16),
             pltpu.VMEM((tokens, hidden), F32),
@@ -346,8 +349,8 @@
             collective_id=0, has_side_effects=True, vmem_limit_bytes=60 * 1024 * 1024
         ),
     )(
-        residual, norm_gain.reshape(1, model), expert_ids, expert_weights,
-        gate_proj, up_proj, down_proj,
+        residual, norm_gain, expert_ids.T, expert_weights.T,
+        gate_proj.transpose(0, 2, 1), up_proj.transpose(0, 2, 1), down_proj,
     )
 
 

time: 63.1 us -> 45.8 us (0.73)
  local copies, waits for them, and re-layouts: 18.6 us -> 1.54 us
    unnamed x5 -> x1, local copies, waits for them, and re-layouts: 17.3 us -> 1.54 us
    reshape x1 -> x0, local copies, waits for them, and re-layouts: 1.31 us -> none  [fused(): norm_gain.reshape(1, model)]
where the time goes in v2:
time: 45.8 us; the launch traced here: 45.6 us
  Pallas kernels  44.1 us (96%)
  local copies, waits for them, and re-layouts  1.54 us (3%)
    pallas_call x1, Pallas kernels, fused(): pl.pallas_call(functools.partial(kernel, line, experts, in_cuts, out_cuts...  44.1 us
    unnamed x1, local copies, waits for them, and re-layouts  1.54 us

profile of v2, /device:TPU:0, one launch (start us, length us, event | category | flops | bytes accessed | tf_op | source)
XLA Modules:
  0.0 45.6 jit_solution(99789454940569959)
XLA Ops:
  0.0 44.1 %shard_map.73 = bf16[16,2880]{1,0:T(8,128)(2,1)} custom-call(bf16[16,2880]{1,0:T(8,128)(2,1)} %res_ref.1, f32[2880]{0:T(1024)} %gain_ref.1, s32[4,16]{1,0:T(4,128)} %bitcast.6, f32[4,16]{1,0:T(4,128)} %bitcast.7, bf16[1,720,2880]{2,1,0:T(8,128)(2,1)} %bitcast.4, bf16[1,720,2880]{2,1,0:T(8,128)(2,1)} %bitcast.5, bf16[1,720,2880]{2,1,0:T(8,128)(2,1)} %down_hbm.1), custom_call_target="tpu_custom_call" | custom-call | tf_op jit(solution)/shard_map/pallas_call | solution.py:315
  44.1 1.5 %copy.9 = bf16[16,2880]{1,0:T(8,128)(2,1)} copy(bf16[16,2880]{1,0:T(8,128)(2,1)} %shard_map.73) | data formatting | bytes 184320

commit v3 on v2

v3 whole, which is shorter than its diff:
```python
import functools

import jax
import jax.numpy as jnp
from jax import lax
from jax.experimental import pallas as pl
from jax.experimental.pallas import tpu as pltpu
from jax.sharding import PartitionSpec as P

BF16 = jnp.bfloat16
F32 = jnp.float32
LANES = 128


def partner(value, axis, bit):
    mask = 2**bit
    pairs = [(source, source ^ mask) for source in range(lax.axis_size(axis))]
    return lax.ppermute(value, axis, pairs)


def expert_half(block, gate_w, up_w, down_w):
    flat = block.reshape(-1, block.shape[-1])
    gate = jnp.dot(flat, gate_w, preferred_element_type=jnp.float32)
    upper = jnp.dot(flat, up_w, preferred_element_type=jnp.float32)
    act = (gate * jax.nn.sigmoid(1.702 * gate) * (upper + 1.0)).astype(jnp.bfloat16)
    out = jnp.dot(act, down_w, preferred_element_type=jnp.float32).astype(jnp.bfloat16)
    return out.reshape(block.shape[:-1] + (down_w.shape[1],))


def slotted(residual, norm_gain, expert_ids, expert_weights, gate_proj, up_proj, down_proj):
    rows, model = residual.shape
    chosen = expert_ids.shape[1]
    devices = lax.axis_size("expert")
    experts = devices // 2
    capacity = 2 * rows * chosen // experts
    half_cap = capacity // 2
    gate_w, up_w, down_w = (gate_proj[0], up_proj[0], down_proj[0])
    x = residual.astype(jnp.float32)
    scale = lax.rsqrt(jnp.mean(x * x, axis=-1, keepdims=True) + 1e-05)
    normed = (x * scale * norm_gain).astype(jnp.bfloat16)
    flat_ids = expert_ids.reshape(rows * chosen)
    onehot = (
        flat_ids[:, None] == lax.broadcasted_iota(jnp.int32, (rows * chosen, experts), 1)
    ).astype(jnp.int32)
    slot = jnp.sum(onehot * jnp.cumsum(onehot, axis=0), axis=1) - 1
    position = flat_ids * capacity + slot
    pick = (
        position[:, None] == lax.broadcasted_iota(jnp.int32, (rows * chosen, experts * capacity), 1)
    ).astype(jnp.float32)
    place_rows = jnp.sum(pick.reshape(rows, chosen, experts * capacity), axis=1)
    send = lax.dot_general(
        place_rows.astype(jnp.bfloat16),
        normed,
        (((0,), (0,)), ((), ())),
        preferred_element_type=jnp.float32,
    )
    send = send.astype(jnp.bfloat16).reshape(experts, capacity, model)
    outgoing = send.reshape(experts, 2, half_cap, model).reshape(devices, half_cap, model)
    arrived = lax.all_to_all(outgoing, "expert", split_axis=0, concat_axis=0, tiled=True)
    other = partner(arrived, "expert", 0)
    both = expert_half(jnp.stack((arrived, other)), gate_w, up_w, down_w)
    returned = partner(both[1], "expert", 0)
    finished = (both[0].astype(jnp.float32) + returned.astype(jnp.float32)).astype(jnp.bfloat16)
    back = lax.all_to_all(finished, "expert", split_axis=0, concat_axis=0, tiled=True)
    results = back.reshape(experts, capacity, model)
    weighted = jnp.sum(
        (pick * expert_weights.reshape(rows * chosen)[:, None]).reshape(
            rows, chosen, experts * capacity
        ),
        axis=1,
    )
    combined = jnp.dot(
        weighted,
        results.reshape(experts * capacity, model).astype(jnp.float32),
        precision=lax.Precision.HIGHEST,
    )
    return (x + combined).astype(jnp.bfloat16)


def cuts(total, shares):
    unit = 2 * LANES
    whole = sum(shares)
    ends = [round(total * sum(shares[: n + 1]) / whole / unit) * unit for n in range(len(shares))]
    ends = sorted(set(min(max(e, unit), total) for e in ends[:-1]) | {total})
    starts = [0] + ends[:-1]
    return [(s, e - s) for s, e in zip(starts, ends) if e > s]


def kernel(
    line, experts, in_cuts, out_cuts,
    res_ref, gain_ref, ids_ref, wts_ref, gate_hbm, up_hbm, down_hbm, out_ref,
    gate_v, up_v, down_v, xg, gacc, uacc, part, core_r, y_s, y_r, z_s, z_r,
    w_sem, d_sem, agz_s, agz_r, agy_s, agy_r, agc_s, agc_r,
    rc_s, rc_r, ry_s, ry_r, rz_s, rz_r,
):
    rows, model = res_ref.shape
    extra = xg.shape[1] - model
    halves, short = 1, rows
    tokens = 4 * line * short
    half, quarter = tokens // 2, tokens // 4
    me = lax.axis_index("expert")
    core = lax.rem(me, 2)
    y = lax.rem(me // 2, 2)
    z = me // 4

    def device(z_, y_, c_):
        return (z_ * 2 + y_) * 2 + c_

    def row(h, z_, y_, c_):
        return pl.multiple_of(((c_ * 2 + y_) * line + z_) * short + h * tokens, short)

    def remote(src, dst, send, recv, target):
        return pltpu.make_async_remote_copy(
            src_ref=src, dst_ref=dst, send_sem=send, recv_sem=recv,
            device_id={"expert": target}, device_id_type=pl.DeviceIdType.MESH,
        )

    if line == 4:
        inner = lax.rem((z + 1) // 2, 2)
        beside = z + 1 - 2 * lax.rem(z, 2)
        skip, mirror = lax.rem(z + 2, 4), 3 - z
        others = [
            beside,
            inner * mirror + (1 - inner) * skip,
            inner * skip + (1 - inner) * mirror,
        ]
    else:
        others = [lax.rem(z + o, line) for o in range(1, line)]
    y_dev = device(z, 1 - y, core)
    c_dev = device(z, y, 1 - core)

    loads = []
    for k, (at, wide) in enumerate(in_cuts):
        pair = []
        for n, (hbm, vmem) in enumerate(((gate_hbm, gate_v), (up_hbm, up_v))):
            copy = pltpu.make_async_copy(
                hbm.at[0, :, pl.ds(at, wide)], vmem.at[:, pl.ds(at, wide)], w_sem.at[k, n]
            )
            copy.start()
            pair.append(copy)
        loads.append(pair)
    down_load = pltpu.make_async_copy(down_hbm.at[0], down_v, d_sem)
    down_load.start()

    barrier = pltpu.get_barrier_semaphore()
    peers = [device(z_, y, core) for z_ in others] + [y_dev, c_dev]
    for peer in peers:
        pl.semaphore_signal(
            barrier, inc=1, device_id={"expert": peer}, device_id_type=pl.DeviceIdType.MESH
        )

    x = res_ref[...].astype(F32)
    scale = lax.rsqrt(jnp.mean(x * x, axis=-1, keepdims=True) + 1e-05)
    normed = (x * scale * gain_ref[...]).astype(BF16)
    named = lax.broadcasted_iota(jnp.int32, (extra, rows), 0)
    high = jnp.zeros((extra, rows), F32)
    low = jnp.zeros((extra, rows), F32)
    for k in range(ids_ref.shape[0]):
        ids = ids_ref[k : k + 1, :]
        high = high + jnp.where(ids == named, wts_ref[k : k + 1, :], 0.0)
        low = low + jnp.where(ids + experts == named, wts_ref[k : k + 1, :], 0.0)
    rest = low - low.astype(BF16).astype(F32)
    shares = jnp.transpose(high + rest).astype(BF16)
    for h in range(halves):
        mine = pl.ds(row(h, z, y, core), short)
        xg[mine, 0:model] = normed[h * short : (h + 1) * short]
        xg[mine, model : model + extra] = shares[h * short : (h + 1) * short]

    pl.semaphore_wait(barrier, len(peers))

    sent = []

    def go(copy):
        copy.start()
        sent.append(copy)

    chunks = len(in_cuts)

    def block(k, z_, y_, c_, count):
        at, wide = in_cuts[k]
        if k == chunks - 1:
            wide = wide + extra
        return xg.at[pl.ds(row(0, z_, y_, c_), count * short), pl.ds(at, wide)]

    for k in range(chunks):
        own = block(k, z, y, core, 1)
        go(remote(own, own, agy_s.at[k, z], agy_r.at[k, z], y_dev))
        for there in others:
            go(remote(own, own, agz_s.at[k, there], agz_r.at[k, z], device(there, y, core)))

    def relay_z(h):
        for there in others:
            got = block(h, there, y, core, 1)
            remote(got, got, agz_s.at[h, there], agz_r.at[h, there], c_dev).wait_recv()
            go(remote(got, got, agy_s.at[h, there], agy_r.at[h, there], y_dev))
        group = block(h, 0, y, core, line)
        go(remote(group, group, agc_s.at[h, 0], agc_r.at[h, 0], c_dev))

    def relay_y(h):
        for there in [z] + others:
            got = block(h, there, 1 - y, core, 1)
            remote(got, got, agy_s.at[h, there], agy_r.at[h, there], y_dev).wait_recv()
        group = block(h, 0, 1 - y, core, line)
        go(remote(group, group, agc_s.at[h, 1], agc_r.at[h, 1], c_dev))

    def arrive(h):
        for n, y_ in enumerate((y, 1 - y)):
            group = block(h, 0, y_, 1 - core, line)
            remote(group, group, agc_s.at[h, n], agc_r.at[h, n], c_dev).wait_recv()

    expert = me // 2

    def multiply(k):
        at, wide = in_cuts[k]
        for n, (vmem, acc) in enumerate(((gate_v, gacc), (up_v, uacc))):
            loads[k][n].wait()
            product = lax.dot_general(
                xg[:, at : at + wide], vmem[:, at : at + wide], (((1,), (1,)), ((), ())),
                preferred_element_type=F32,
            )
            if k == 0:
                acc[...] = product
            else:
                acc[...] += product

    def hidden():
        gate = gacc[...]
        act = (gate * jax.nn.sigmoid(1.702 * gate) * (uacc[...] + 1.0)).astype(BF16)
        lanes = lax.broadcasted_iota(jnp.int32, (tokens, extra), 1)
        ours = jnp.logical_or(lanes == expert, lanes == expert + experts)
        weight = jnp.sum(
            jnp.where(ours, xg[:, model : model + extra].astype(F32), 0.0),
            axis=1, keepdims=True,
        )
        return act, weight

    my_half = core * half
    its_half = (1 - core) * half
    my_y = y * quarter
    its_y = (1 - y) * quarter

    def at_row(value, unit):
        return pl.multiple_of(value, unit)

    def core_copy(h, j):
        at, wide = out_cuts[j]
        cols = pl.ds(at, wide)
        return remote(
            part.at[pl.ds(at_row(its_half + h * tokens, half), half), cols],
            core_r.at[pl.ds(h * half, half), cols],
            rc_s.at[h, j], rc_r.at[h, j], c_dev,
        )

    def y_copy(h, j):
        at, wide = out_cuts[j]
        spot = (pl.ds(h * quarter, quarter), pl.ds(at, wide))
        return remote(y_s.at[spot], y_r.at[spot], ry_s.at[h, j], ry_r.at[h, j], y_dev)

    def z_copy(h, j, there):
        at, wide = out_cuts[j]
        cols = pl.ds(at, wide)
        return remote(
            z_s.at[pl.ds(at_row(h * quarter + there * short, short), short), cols],
            z_r.at[pl.ds(at_row(h * quarter + z * short, short), short), cols],
            rz_s.at[h, j, there], rz_r.at[h, j, z], device(there, y, core),
        )

    def z_arrival(h, j, there):
        at, wide = out_cuts[j]
        spot = (pl.ds(at_row(h * quarter + there * short, short), short), pl.ds(at, wide))
        return remote(
            z_r.at[spot], z_r.at[spot], rz_s.at[h, j, there], rz_r.at[h, j, there], c_dev
        )

    def first(h, j, act, weight):
        at, wide = out_cuts[j]
        product = jnp.dot(act, down_v[:, at : at + wide], preferred_element_type=F32)
        part[h * tokens : (h + 1) * tokens, at : at + wide] = (product * weight).astype(BF16)
        go(core_copy(h, j))

    def pair_sum(h, j, which):
        at, wide = out_cuts[j]
        theirs = core_r[pl.ds(at_row(h * half + which, quarter), quarter), at : at + wide]
        here = part[
            pl.ds(at_row(h * tokens + my_half + which, quarter), quarter), at : at + wide
        ]
        return theirs.astype(F32) + here.astype(F32)

    def second(h, j):
        at, wide = out_cuts[j]
        core_copy(h, j).wait_recv()
        y_s[h * quarter : (h + 1) * quarter, at : at + wide] = pair_sum(h, j, its_y).astype(BF16)
        go(y_copy(h, j))

    def third(h, j):
        at, wide = out_cuts[j]
        total = pair_sum(h, j, my_y)
        y_copy(h, j).wait_recv()
        span = slice(h * quarter, (h + 1) * quarter)
        total = total + y_r[span, at : at + wide].astype(F32)
        z_s[span, at : at + wide] = total.astype(BF16)
        for there in others[::-1]:
            go(z_copy(h, j, there))

    def fourth(h, j):
        at, wide = out_cuts[j]
        own = pl.ds(at_row(h * quarter + z * short, short), short)
        total = z_s[own, at : at + wide].astype(F32)
        for there in others:
            z_arrival(h, j, there).wait_recv()
            spot = pl.ds(at_row(h * quarter + there * short, short), short)
            total = total + z_r[spot, at : at + wide].astype(F32)
        span = slice(h * short, (h + 1) * short)
        out_ref[span, at : at + wide] = (
            res_ref[span, at : at + wide].astype(F32) + total
        ).astype(BF16)

    pieces = range(len(out_cuts))
    relay_z(0)
    for k in range(chunks):
        if k + 1 < chunks:
            relay_z(k + 1)
        relay_y(k)
        arrive(k)
        multiply(k)
    act, weight = hidden()
    down_load.wait()
    lags = (0, 1, 3)
    for step in range(len(out_cuts) + lags[-1]):
        for lag, stage in zip(lags, (first, second, third)):
            if 0 <= step - lag < len(out_cuts):
                if stage is first:
                    first(0, step, act, weight)
                else:
                    stage(0, step - lag)
    for h in range(halves):
        for j in pieces:
            fourth(h, j)
    for copy in sent:
        copy.wait_send()


def fused(residual, norm_gain, expert_ids, expert_weights, gate_proj, up_proj, down_proj):
    rows, model = residual.shape
    hidden = gate_proj.shape[2]
    devices = lax.axis_size("expert")
    experts = devices // 2
    line = devices // 4
    halves = 1
    in_cuts = cuts(model, (4, 4, 3))
    ins = len(in_cuts)
    tokens = rows * devices
    width = -(-(model + 2 * experts) // LANES) * LANES
    out_cuts = cuts(model, (2, 3, 3, 2, 1))
    outs = len(out_cuts)
    vmem = pl.BlockSpec(memory_space=pltpu.VMEM)
    hbm = pl.BlockSpec(memory_space=pl.ANY)
    dma = pltpu.SemaphoreType.DMA
    return pl.pallas_call(
        functools.partial(kernel, line, experts, in_cuts, out_cuts),
        out_shape=jax.ShapeDtypeStruct((rows, model), BF16),
        in_specs=[vmem] * 4 + [hbm] * 3,
        out_specs=vmem,
        scratch_shapes=[
            pltpu.VMEM((hidden, model), BF16),
            pltpu.VMEM((hidden, model), BF16),
            pltpu.VMEM((hidden, model), BF16),
            pltpu.VMEM((tokens, width), BF16),
            pltpu.VMEM((tokens, hidden), F32),
            pltpu.VMEM((tokens, hidden), F32),
            pltpu.VMEM((tokens, model), BF16),
            pltpu.VMEM((tokens // 2, model), BF16),
            pltpu.VMEM((tokens // 4, model), BF16),
            pltpu.VMEM((tokens // 4, model), BF16),
            pltpu.VMEM((tokens // 4, model), BF16),
            pltpu.VMEM((tokens // 4, model), BF16),
            dma((ins, 2)),
            dma,
            dma((ins, line)),
            dma((ins, line)),
            dma((ins, line)),
            dma((ins, line)),
            dma((ins, 2)),
            dma((ins, 2)),
            dma((halves, outs)),
            dma((halves, outs)),
            dma((halves, outs)),
            dma((halves, outs)),
            dma((halves, outs, line)),
            dma((halves, outs, line)),
        ],
        compiler_params=pltpu.CompilerParams(
            collective_id=0, has_side_effects=True, vmem_limit_bytes=60 * 1024 * 1024
        ),
    )(
        residual, norm_gain, expert_ids.T, expert_weights.T,
        gate_proj.transpose(0, 2, 1), up_proj.transpose(0, 2, 1), down_proj,
    )


def body(residual, norm_gain, expert_ids, expert_weights, gate_proj, up_proj, down_proj):
    rows = residual.shape[0]
    devices = lax.axis_size("expert")
    capacity = 4 * rows * expert_ids.shape[1] // devices
    dense = capacity >= rows and devices % 4 == 0
    form = fused if dense else slotted
    return form(
        residual, norm_gain, expert_ids, expert_weights, gate_proj, up_proj, down_proj
    )


def solution(mesh):
    in_specs = (
        P(("groups", "expert"), None),
        P(),
        P(("groups", "expert"), None),
        P(("groups", "expert"), None),
        P("expert", None, None),
        P("expert", None, None),
        P("expert", None, None),
    )
    out_specs = P(("groups", "expert"), None)
    return jax.shard_map(body, mesh=mesh, in_specs=in_specs, out_specs=out_specs, check_vma=False)
```

time: 45.8 us -> 42.8 us (0.934)
  Pallas kernels: 44.1 us -> 41 us
    pallas_call x1, Pallas kernels: 44.1 us -> 41 us  [fused(): pl.pallas_call(functools.partial(kernel, line, experts, in_cuts, out_cuts...]
where the time goes in v3:
time: 42.8 us; the launch traced here: 42.6 us
  Pallas kernels  41 us (96%)
  local copies, waits for them, and re-layouts  1.54 us (4%)
    pallas_call x1, Pallas kernels, fused(): pl.pallas_call(functools.partial(kernel, line, experts, in_cuts, out_cuts...  41 us
    unnamed x1, local copies, waits for them, and re-layouts  1.54 us

profile of v3, /device:TPU:0, one launch (start us, length us, event | category | flops | bytes accessed | tf_op | source)
XLA Modules:
  0.0 42.6 jit_solution(13062731753264351683)
XLA Ops:
  0.0 41.0 %shard_map.73 = bf16[16,2880]{1,0:T(8,128)(2,1)} custom-call(bf16[16,2880]{1,0:T(8,128)(2,1)} %res_ref.1, f32[2880]{0:T(1024)} %gain_ref.1, s32[4,16]{1,0:T(4,128)} %bitcast.6, f32[4,16]{1,0:T(4,128)} %bitcast.7, bf16[1,720,2880]{2,1,0:T(8,128)(2,1)} %bitcast.4, bf16[1,720,2880]{2,1,0:T(8,128)(2,1)} %bitcast.5, bf16[1,720,2880]{2,1,0:T(8,128)(2,1)} %down_hbm.1), custom_call_target="tpu_custom_call" | custom-call | tf_op jit(solution)/shard_map/pallas_call | solution.py:359
  41.0 1.5 %copy.9 = bf16[16,2880]{1,0:T(8,128)(2,1)} copy(bf16[16,2880]{1,0:T(8,128)(2,1)} %shard_map.73) | data formatting | bytes 184320

commit v4 on v3

--- a/solution.py
+++ b/solution.py
@@ -90,7 +90,7 @@
     line, experts, in_cuts, out_cuts,
     res_ref, gain_ref, ids_ref, wts_ref, gate_hbm, up_hbm, down_hbm, out_ref,
     gate_v, up_v, down_v, xg, gacc, uacc, part, core_r, y_s, y_r, z_s, z_r,
-    w_sem, d_sem, agz_s, agz_r, agy_s, agy_r, agc_s, agc_r,
+    w_sem, d_sem, agl_s, agr_s, agz_r, agy_s, agy_r, agc_s, agc_r,
     rc_s, rc_r, ry_s, ry_r, rz_s, rz_r,
 ):
     rows, model = res_ref.shape
@@ -143,11 +143,19 @@
     down_load.start()
 
     barrier = pltpu.get_barrier_semaphore()
-    peers = [device(z_, y, core) for z_ in others] + [y_dev, c_dev]
-    for peer in peers:
+    last = line - 1
+    has_left = (z + last) // line
+    has_right = (2 * last - z) // line
+
+    def greet(peer):
         pl.semaphore_signal(
             barrier, inc=1, device_id={"expert": peer}, device_id_type=pl.DeviceIdType.MESH
         )
+
+    greet(y_dev)
+    greet(c_dev)
+    pl.when(z > 0)(lambda: greet(device(z - 1, y, core)))
+    pl.when(z < last)(lambda: greet(device(z + 1, y, core)))
 
     x = res_ref[...].astype(F32)
     scale = lax.rsqrt(jnp.mean(x * x, axis=-1, keepdims=True) + 1e-05)
@@ -166,7 +174,7 @@
         xg[mine, 0:model] = normed[h * short : (h + 1) * short]
         xg[mine, model : model + extra] = shares[h * short : (h + 1) * short]
 
-    pl.semaphore_wait(barrier, len(peers))
+    pl.semaphore_wait(barrier, 2 + has_left + has_right)
 
     sent = []
 
@@ -182,31 +190,62 @@
             wide = wide + extra
         return xg.at[pl.ds(row(0, z_, y_, c_), count * short), pl.ds(at, wide)]
 
+    def pass_left(k, z_):
+        at = block(k, z_, y, core, 1)
+        return remote(at, at, agl_s.at[k, z_], agz_r.at[k, z_], device(z - 1, y, core))
+
+    def pass_right(k, z_):
+        at = block(k, z_, y, core, 1)
+        return remote(at, at, agr_s.at[k, z_], agz_r.at[k, z_], device(z + 1, y, core))
+
+    def pass_y(k, z_):
+        at = block(k, z_, y, core, 1)
+        return remote(at, at, agy_s.at[k, z_], agy_r.at[k, z_], y_dev)
+
+    def from_right(k, d):
+        pass_left(k, z + d).wait_recv()
+        pass_y(k, z + d).start()
+        pl.when(z > 0)(lambda: pass_left(k, z + d).start())
+
+    def from_left(k, d):
+        pass_right(k, z - d).wait_recv()
+        pass_y(k, z - d).start()
+        pl.when(z < last)(lambda: pass_right(k, z - d).start())
+
     for k in range(chunks):
-        own = block(k, z, y, core, 1)
-        go(remote(own, own, agy_s.at[k, z], agy_r.at[k, z], y_dev))
-        for there in others:
-            go(remote(own, own, agz_s.at[k, there], agz_r.at[k, z], device(there, y, core)))
-
-    def relay_z(h):
-        for there in others:
-            got = block(h, there, y, core, 1)
-            remote(got, got, agz_s.at[h, there], agz_r.at[h, there], c_dev).wait_recv()
-            go(remote(got, got, agy_s.at[h, there], agy_r.at[h, there], y_dev))
-        group = block(h, 0, y, core, line)
-        go(remote(group, group, agc_s.at[h, 0], agc_r.at[h, 0], c_dev))
-
-    def relay_y(h):
-        for there in [z] + others:
-            got = block(h, there, 1 - y, core, 1)
-            remote(got, got, agy_s.at[h, there], agy_r.at[h, there], y_dev).wait_recv()
-        group = block(h, 0, 1 - y, core, line)
-        go(remote(group, group, agc_s.at[h, 1], agc_r.at[h, 1], c_dev))
-
-    def arrive(h):
+        pass_y(k, z).start()
+        pl.when(z > 0)(lambda: pass_left(k, z).start())
+        pl.when(z < last)(lambda: pass_right(k, z).start())
+
+    def line_step(d, k):
+        pl.when(z + d <= last)(lambda: from_right(k, d))
+        pl.when(z - d >= 0)(lambda: from_left(k, d))
+
+    def core_group(k, n):
+        group = block(k, 0, y if n == 0 else 1 - y, core, line)
+        go(remote(group, group, agc_s.at[k, n], agc_r.at[k, n], c_dev))
+
+    def relay_y(k):
+        for there in range(line):
+            got = block(k, there, 1 - y, core, 1)
+            remote(got, got, agy_s.at[k, there], agy_r.at[k, there], y_dev).wait_recv()
+        core_group(k, 1)
+
+    def arrive(k):
         for n, y_ in enumerate((y, 1 - y)):
-            group = block(h, 0, y_, 1 - core, line)
-            remote(group, group, agc_s.at[h, n], agc_r.at[h, n], c_dev).wait_recv()
+            group = block(k, 0, y_, 1 - core, line)
+            remote(group, group, agc_s.at[k, n], agc_r.at[k, n], c_dev).wait_recv()
+
+    def drain_gather():
+        for k in range(chunks):
+            for z_ in range(line):
+                pass_y(k, z_).wait_send()
+                pl.when(jnp.logical_and(z > 0, z <= z_))(
+                    lambda: pass_left(k, z_).wait_send()
+                )
+                pl.when(jnp.logical_and(z < last, z >= z_))(
+                    lambda: pass_right(k, z_).wait_send()
+                )
 
     expert = me // 2
 
@@ -316,11 +355,14 @@
         ).astype(BF16)
 
     pieces = range(len(out_cuts))
-    relay_z(0)
+    for d in range(1, line):
+        for k in range(chunks):
+            line_step(d, k)
+            if d == last:
+                core_group(k, 0)
     for k in range(chunks):
-        if k + 1 < chunks:
-            relay_z(k + 1)
         relay_y(k)
+    for k in range(chunks):
         arrive(k)
         multiply(k)
     act, weight = hidden()
@@ -336,6 +378,7 @@
     for h in range(halves):
         for j in pieces:
             fourth(h, j)
+    drain_gather()
     for copy in sent:
         copy.wait_send()
 
@@ -380,6 +423,7 @@
             dma((ins, line)),
             dma((ins, line)),
             dma((ins, line)),
+            dma((ins, line)),
             dma((ins, 2)),
             dma((ins, 2)),
             dma((halves, outs)),

time: 42.8 us -> 40.8 us (0.953)
  Pallas kernels: 41 us -> 39.1 us
    pallas_call x1, Pallas kernels: 41 us -> 39.1 us  [fused(): pl.pallas_call(functools.partial(kernel, line, experts, in_cuts, out_cuts...]
where the time goes in v4:
time: 40.8 us; the launch traced here: 40.6 us
  Pallas kernels  39.1 us (96%)
  local copies, waits for them, and re-layouts  1.54 us (4%)
    pallas_call x1, Pallas kernels, fused(): pl.pallas_call(functools.partial(kernel, line, experts, in_cuts, out_cuts...  39.1 us
    unnamed x1, local copies, waits for them, and re-layouts  1.54 us

profile of v4, /device:TPU:0, one launch (start us, length us, event | category | flops | bytes accessed | tf_op | source)
XLA Modules:
  0.0 40.6 jit_solution(5074138144492457515)
XLA Ops:
  0.0 39.1 %shard_map.73 = bf16[16,2880]{1,0:T(8,128)(2,1)} custom-call(bf16[16,2880]{1,0:T(8,128)(2,1)} %res_ref.1, f32[2880]{0:T(1024)} %gain_ref.1, s32[4,16]{1,0:T(4,128)} %bitcast.6, f32[4,16]{1,0:T(4,128)} %bitcast.7, bf16[1,720,2880]{2,1,0:T(8,128)(2,1)} %bitcast.4, bf16[1,720,2880]{2,1,0:T(8,128)(2,1)} %bitcast.5, bf16[1,720,2880]{2,1,0:T(8,128)(2,1)} %down_hbm.1), custom_call_target="tpu_custom_call" | custom-call | tf_op jit(solution)/shard_map/pallas_call | solution.py:402
  39.1 1.5 %copy.9 = bf16[16,2880]{1,0:T(8,128)(2,1)} copy(bf16[16,2880]{1,0:T(8,128)(2,1)} %shard_map.73) | data formatting | bytes 184320

commit v5 on v4

--- a/solution.py
+++ b/solution.py
@@ -390,7 +390,7 @@
     experts = devices // 2
     line = devices // 4
     halves = 1
-    in_cuts = cuts(model, (4, 4, 3))
+    in_cuts = cuts(model, (6, 5))
     ins = len(in_cuts)
     tokens = rows * devices
     width = -(-(model + 2 * experts) // LANES) * LANES

time: 40.8 us -> 40.9 us (level)
  no operation moved by 1% of the time
where the time goes in v5:
time: 40.9 us; the launch traced here: 40.7 us
  Pallas kernels  39.1 us (96%)
  local copies, waits for them, and re-layouts  1.54 us (4%)
    pallas_call x1, Pallas kernels, fused(): pl.pallas_call(functools.partial(kernel, line, experts, in_cuts, out_cuts...  39.1 us
    unnamed x1, local copies, waits for them, and re-layouts  1.54 us

profile of v5, /device:TPU:0, one launch (start us, length us, event | category | flops | bytes accessed | tf_op | source)
XLA Modules:
  0.0 40.7 jit_solution(9488021232716252877)
XLA Ops:
  0.0 39.1 %shard_map.73 = bf16[16,2880]{1,0:T(8,128)(2,1)} custom-call(bf16[16,2880]{1,0:T(8,128)(2,1)} %res_ref.1, f32[2880]{0:T(1024)} %gain_ref.1, s32[4,16]{1,0:T(4,128)} %bitcast.6, f32[4,16]{1,0:T(4,128)} %bitcast.7, bf16[1,720,2880]{2,1,0:T(8,128)(2,1)} %bitcast.4, bf16[1,720,2880]{2,1,0:T(8,128)(2,1)} %bitcast.5, bf16[1,720,2880]{2,1,0:T(8,128)(2,1)} %down_hbm.1), custom_call_target="tpu_custom_call" | custom-call | tf_op jit(solution)/shard_map/pallas_call | solution.py:402
  39.1 1.5 %copy.9 = bf16[16,2880]{1,0:T(8,128)(2,1)} copy(bf16[16,2880]{1,0:T(8,128)(2,1)} %shard_map.73) | data formatting | bytes 184320
